TPU v7x, 128 devices: a whole 4x4x4 slice. The times are simulated.
128 devices in a mesh: gx: 8 (over z, x_hi), gy: 16 (over x_lo, y, core).
Axes of the slice: x: 4 (x_hi: 2, x_lo: 2; x = x_hi * 2 + x_lo), y: 4, z: 4, core: 2. Of those that a mesh axis runs over, the one named last changes fastest.
Arguments:
- ensemble: float32 [192, 384, 6, 128], P('gx', 'gy'), may hold values from -6 to 6
- cfl_ratio_primary_axis: float32 [192, 384, 6], P('gx', 'gy'), may hold values from -0.35 to 0.35
- cfl_ratio_secondary_axis: float32 [192, 384, 6], P('gx', 'gy'), may hold values from -0.35 to 0.35
- spreading_ratio: float32 [192, 384, 6], P('gx', 'gy'), may hold values from 0.02 to 0.07
- obs_owner: int32 [1024], replicated, may hold values from 0 to 127
- obs_local: int32 [1024], replicated, may hold values from 0 to 3455
- batch_order: int32 [1024], replicated, may hold values from 0 to 1023, each once
- obs_reach: int32 [1024], replicated, may hold values from 24 to 72
- obs_value: float32 [1024], replicated, may hold values from -6 to 6
- obs_variance: float32 [1024], replicated, may hold values from 0.25 to 4
- obs_noise: float32 [1024, 128], replicated, may hold values from -6 to 6
Outputs:
- analysis: float32 [192, 384, 6, 128], P('gx', 'gy')
All inputs are finite; a program needn't handle non-finite values.
Results may differ from a plain program's by a relative error of at most 0.0001.
Values sent between devices are 32-bit elements; how exact they have to be, the bound alone decides.
A program may use at most 64 MiB of HBM per device.

v0:
```python
import functools

import jax
import jax.numpy as jnp
from jax import lax
from jax.experimental import pallas as pl
from jax.experimental.pallas import tpu as pltpu
from jax.sharding import PartitionSpec as P

OB = 64
QUICK = 6.5
WIDE = 63.0
LONG = 6
MESH = pl.DeviceIdType.MESH
F32 = jnp.float32
BF16 = jnp.bfloat16


def floor_div(x, n, top):
    shift = 1
    while any((v * -(-(1 << shift) // n)) >> shift != v // n for v in range(top)):
        shift += 1
    return (x * -(-(1 << shift) // n)) >> shift


def thirds(x):
    high = x.astype(BF16).astype(F32)
    rest = x - high
    mid = rest.astype(BF16).astype(F32)
    return [high, mid, rest - mid]


def exchange(
    x_ref, cx_ref, cy_ref, kd_ref, owner_ref, local_ref, reach_ref, value_ref, variance_ref, order_ref, noise_hbm,
    state_hbm, y_ref, w_hbm, rows_c_hbm, rows_i_hbm,
    field_ref, mid_ref, wide_ref, flip_ref, cols_ref, rows_in, cols_in,
    noise_ref, w_ref, rows_c, rows_i, part_ref, half_ref, sum_ref, slots_ref, ints_ref, floats_ref,
    place_s, code_s, inv_s, shift_s, halo_send, halo_recv, send_sem, recv_sem, copy_sem, table_sem,
):
    strip, members = rows_in.shape[2:]
    block_y = cx_ref.shape[1]
    levels = strip // block_y
    block_x = cx_ref.shape[0] // levels
    lines = block_x * levels
    size = lines * block_y
    gx, gy = lax.axis_index("gx"), lax.axis_index("gy")
    nx, ny = lax.axis_size("gx"), lax.axis_size("gy")
    west, east = (lax.rem(gx + nx - 1, nx), gy), (lax.rem(gx + 1, nx), gy)
    south, north = (gx, lax.rem(gy + ny - 1, ny)), (gx, lax.rem(gy + 1, ny))
    count = part_ref.shape[0]
    half = count // 2
    my = ny // 2
    chips = nx * my
    piece = half // chips
    core = lax.rem(gy, 2)
    chip = gx * my + gy // 2
    partner = (gx, gy + 1 - 2 * core)

    def others(visit):
        def line(a, start):
            ox = lax.rem(gx + a, nx)
            for b in range(start, my):
                oy = lax.rem(gy // 2 + b, my)
                visit(ox * my + oy, (ox, oy * 2 + core))

        line(0, 1)

        def body(a, _):
            line(a, 0)
            return 0

        lax.fori_loop(1, nx, body, 0)

    barrier = pltpu.get_barrier_semaphore()

    def greet(_, device):
        pl.semaphore_signal(barrier, inc=1, device_id=device, device_id_type=MESH)

    for device in (west, east, south, north, partner):
        greet(None, device)
    others(greet)
    fetch = pltpu.make_async_copy(noise_hbm, noise_ref, copy_sem.at[0])
    fetch.start()
    from_west = jnp.where(gx > 0, 1.0, 0.0).astype(F32)
    from_east = jnp.where(gx < nx - 1, 1.0, 0.0).astype(F32)
    from_south = jnp.where(gy > 0, 1.0, 0.0).astype(F32)
    from_north = jnp.where(gy < ny - 1, 1.0, 0.0).astype(F32)

    def pack(field, turn):
        cols_ref[turn, 0] = field[pl.ds(0, lines, stride=block_y), :]
        cols_ref[turn, 1] = field[pl.ds(block_y - 1, lines, stride=block_y), :]

    def sends(field, turn):
        last = (block_x - 1) * strip
        plan = (
            (field.at[pl.ds(last, strip)], rows_in.at[turn, 0], east),
            (field.at[pl.ds(0, strip)], rows_in.at[turn, 1], west),
            (cols_ref.at[turn, 1], cols_in.at[turn, 0], north),
            (cols_ref.at[turn, 0], cols_in.at[turn, 1], south),
        )
        return [
            pltpu.make_async_remote_copy(
                src_ref=source,
                dst_ref=target,
                send_sem=halo_send.at[turn, i],
                recv_sem=halo_recv.at[turn, i],
                device_id=device,
                device_id_type=MESH,
            )
            for i, (source, target, device) in enumerate(plan)
        ]

    def rows_of(i, l):
        return pl.ds(pl.multiple_of((i * levels + l) * block_y, block_y), block_y)

    def strip_of(field, i):
        return [field[rows_of(i, l), :] for l in range(levels)]

    zero = jnp.zeros((1, members), F32)

    def advance(i, centre, left, right, target):
        for l in range(levels):
            w = [wide_ref[k, rows_of(i, l), :] for k in range(5)]
            c = centre[l]
            new = w[0] * c + w[1] * left[l] + w[2] * right[l]
            new = new + w[3] * jnp.concatenate([zero, c[:-1]], axis=0)
            new = new + w[4] * jnp.concatenate([c[1:], zero], axis=0)
            target[rows_of(i, l), :] = new

    def inside(field, target):
        def inner(i, _):
            advance(i, strip_of(field, i), strip_of(field, i - 1), strip_of(field, i + 1), target)
            return 0

        lax.fori_loop(1, block_x - 1, inner, 0)

    def border(copies, field, target, turn):
        copies[0].wait_recv()
        left = [rows_in[turn, 0, pl.ds(l * block_y, block_y), :] * from_west for l in range(levels)]
        advance(0, strip_of(field, 0), left, strip_of(field, 1), target)
        copies[1].wait_recv()
        right = [rows_in[turn, 1, pl.ds(l * block_y, block_y), :] * from_east for l in range(levels)]
        last = block_x - 1
        advance(last, strip_of(field, last), strip_of(field, last - 1), right, target)
        for side, (at, here) in enumerate(((0, from_south), (block_y - 1, from_north))):
            copies[2 + side].wait_recv()
            rows = pl.ds(at, lines, stride=block_y)
            target[rows, :] = target[rows, :] + wide_ref[3 + side, rows, :] * (cols_in[turn, side] * here)

    pack(x_ref, 0)
    pl.semaphore_wait(barrier, chips + 4)
    first = sends(x_ref, 0)
    for copy in first:
        copy.start()

    def flip(i, _):
        rows = pl.ds(i, levels, stride=block_x)
        cx, cy, kd = cx_ref[rows, :], cy_ref[rows, :], kd_ref[rows, :]
        w1, w2 = kd + jnp.maximum(cx, 0.0), kd - jnp.minimum(cx, 0.0)
        w3, w4 = kd + jnp.maximum(cy, 0.0), kd - jnp.minimum(cy, 0.0)
        packed = jnp.concatenate([1.0 - (w1 + w2 + w3 + w4), w1, w2, w3, w4], axis=0)
        packed = jnp.concatenate(thirds(packed), axis=0)
        at = pl.ds(pl.multiple_of(i * block_y, block_y), block_y)
        flip_ref[at, pl.ds(0, 15 * levels)] = packed.T
        return 0

    lax.fori_loop(0, block_x, flip, 0, unroll=4)
    kinds = 5 * levels
    r = lax.broadcasted_iota(jnp.int32, (3 * kinds, members), 0)
    pick = [((r == k) | (r == k + kinds) | (r == k + 2 * kinds)).astype(F32).astype(BF16) for k in range(kinds)]
    pair = 2 * block_y

    def widen(n, _):
        left = flip_ref[pl.ds(pl.multiple_of(n * pair, pair), pair), pl.ds(0, 3 * kinds)].astype(BF16)
        for k in range(0, kinds, 2):
            right = jnp.concatenate(pick[k : k + 2], axis=1)
            spread_out = jnp.dot(left, right, preferred_element_type=F32)
            for u in range(2):
                for v in range(2):
                    kind, l = divmod(k + v, levels)
                    piece_out = spread_out[u * block_y : (u + 1) * block_y, v * members : (v + 1) * members]
                    wide_ref[kind, rows_of(n * 2 + u, l), :] = piece_out
        return 0

    lax.fori_loop(0, block_x // 2, widen, 0)
    local, owner = local_ref[...], owner_ref[...]
    ix = floor_div(local, block_y * levels, size)
    rest = local - ix * (block_y * levels)
    iy = floor_div(rest, levels, block_y * levels)
    lev = rest - iy * levels
    ox = floor_div(owner, ny, nx * ny)
    oy = owner - ox * ny
    mine = owner == gx * ny + gy
    ints_ref[0] = jnp.where(mine, (ix * levels + lev) * block_y + iy, size)
    px = (ox - gx) * block_x + ix + nx * block_x
    py = (oy - gy) * block_y + iy + ny * block_y
    ints_ref[1] = (px * 1024 + py) * 128 + reach_ref[...]
    inv = lax.rsqrt(variance_ref[...])
    floats_ref[0] = inv
    floats_ref[1] = value_ref[...] * inv
    field_ref[pl.ds(size, 8), :] = jnp.zeros((8, members), F32)
    width = ints_ref.shape[2]
    tables = [
        pltpu.make_async_copy(source.at[r], target.at[pl.ds(r * width, width)], table_sem.at[i, r])
        for i, (source, target) in enumerate(
            ((ints_ref.at[0], place_s), (ints_ref.at[1], code_s), (floats_ref.at[0], inv_s), (floats_ref.at[1], shift_s))
        )
        for r in range(count // width)
    ]
    for table in tables:
        table.start()
    inside(x_ref, mid_ref)
    border(first, x_ref, mid_ref, 0)
    pack(mid_ref, 1)
    second = sends(mid_ref, 1)
    for copy in second:
        copy.start()
    inside(mid_ref, field_ref)
    fetch.wait()
    for table in tables:
        table.wait()
    full = (1, members)

    def look(ref, o):
        return ref[o]

    def prepare(g, _):
        for u in range(8):
            k = g * 8 + u
            o = order_ref[k]
            at = pl.ds(k, 1)
            w_ref[at, :] = noise_ref[pl.ds(o, 1), :] + jnp.full(full, look(shift_s, o))
            rows_c[at, :] = jnp.full(full, look(code_s, o))
            rows_i[at, :] = jnp.full(full, look(inv_s, o))
        return 0

    groups = count // 8
    lax.fori_loop(0, groups // 8, prepare, 0)
    border(second, mid_ref, field_ref, 1)
    keep = pltpu.make_async_copy(field_ref, state_hbm, copy_sem.at[0])
    keep.start()

    def pick_rows(base):
        def body(g, _):
            for u in range(8):
                k = base + g * 8 + u
                part_ref[pl.ds(k, 1), :] = field_ref[pl.ds(look(place_s, order_ref[k]), 1), :]
            return 0

        lax.fori_loop(0, half // 8, body, 0)

    mine = pl.ds(pl.multiple_of(core * half, half), half)
    other = pl.ds(pl.multiple_of((1 - core) * half, half), half)
    pick_rows((1 - core) * half)
    swap = pltpu.make_async_remote_copy(
        src_ref=part_ref.at[other], dst_ref=half_ref, send_sem=send_sem.at[0], recv_sem=recv_sem.at[0],
        device_id=partner, device_id_type=MESH,
    )
    swap.start()
    pick_rows(core * half)
    swap.wait_recv()
    sum_ref[...] = (part_ref[mine, :] + half_ref[...]).reshape(sum_ref.shape)

    def scatter(t, device):
        pltpu.make_async_remote_copy(
            src_ref=sum_ref.at[t], dst_ref=slots_ref.at[chip], send_sem=send_sem.at[1], recv_sem=recv_sem.at[1],
            device_id=device, device_id_type=MESH,
        ).start()

    others(scatter)
    slots_ref[chip] = sum_ref[chip]
    lax.fori_loop(groups // 8, groups // 2, prepare, 0)
    some = slots_ref.at[pl.ds(0, chips - 1)]
    pltpu.make_async_copy(some, some, recv_sem.at[1]).wait()
    own = pl.ds(pl.multiple_of(core * half + chip * piece, piece), piece)
    y_ref[own, :] = jnp.sum(slots_ref[...], axis=0)

    def gather(t, device):
        pltpu.make_async_remote_copy(
            src_ref=y_ref.at[own], dst_ref=y_ref.at[own], send_sem=send_sem.at[2], recv_sem=recv_sem.at[2],
            device_id=device, device_id_type=MESH,
        ).start()

    others(gather)
    lax.fori_loop(groups // 2, groups, prepare, 0)
    stores = [
        pltpu.make_async_copy(source, target, copy_sem.at[1 + i])
        for i, (source, target) in enumerate(((w_ref, w_hbm), (rows_c, rows_c_hbm), (rows_i, rows_i_hbm)))
    ]
    for store in stores:
        store.start()
    pltpu.make_async_copy(some, some, recv_sem.at[2]).wait()
    share = pltpu.make_async_remote_copy(
        src_ref=y_ref.at[mine], dst_ref=y_ref.at[mine], send_sem=send_sem.at[3], recv_sem=recv_sem.at[3],
        device_id=partner, device_id_type=MESH,
    )
    share.start()
    for copy in first + second:
        copy.wait_send()
    swap.wait_send()
    keep.wait()
    for store in stores:
        store.wait()
    pltpu.make_async_copy(some, some, send_sem.at[1]).wait()
    pltpu.make_async_copy(some, some, send_sem.at[2]).wait()
    share.wait()


def split(x):
    high = x.astype(BF16)
    return high, (x - high.astype(F32)).astype(BF16)


def wide(x):
    return jnp.concatenate(split(x), axis=1)


def project(side, x):
    pair = lax.dot_general(wide(x), side, (((1,), (1,)), ((), ())), preferred_element_type=F32)
    half = pair.shape[1] // 2
    return pair[:, :half] + pair[:, half:]


def spread(solved, g):
    return jnp.dot(wide(g), solved, preferred_element_type=F32)


def stack_solved(v, scale):
    high, low = split(v * scale)
    return jnp.concatenate([high, low, high, low], axis=0)


def sharpen(r, v, t, eye, last):
    t = 2.0 * t * t - 1.0
    back = 1.0 / t
    gain = 1.0 + back
    rh, rl = split(r)
    vh, vl = split(v)
    left = jnp.concatenate([rh, rl], axis=1)
    head = jnp.concatenate([rh, vh], axis=1)
    tail = jnp.concatenate([rl, vl], axis=1)
    right = jnp.concatenate([head, tail, head, tail], axis=0)
    prod = jnp.dot(left, right, preferred_element_type=F32)
    v = gain * (v + prod[:, 2 * OB :])
    r = None if last else gain * prod[:, : 2 * OB] - back * eye
    return r, v, t


def begin(p, rhs, norm, eye):
    c = 1.0 + jnp.maximum(norm, 0.0625)
    top = c + 1.0
    alpha = 2.0 / top
    return ((c - 1.0) / top) * eye - alpha * p, alpha * rhs, top / (c - 1.0)


def hinted(x):
    return x if isinstance(x, int) else pl.multiple_of(x, OB)


def assimilate(
    span_x, span_y,
    shape,
    rows_c, rows_i, y_in, w_ref, x_hbm, out_hbm,
    rows_x, rows_y, rows_r, y_ref, t_ref, v_ref, cur_ref, side_ref, solved_ref, lanes_ref,
    first_ref, pair_ref, mix_ref, back_ref, both_ref, out_ref, copy_sem,
):
    block_x, levels, block_y, members = shape
    size = block_x * levels * block_y
    load = pltpu.make_async_copy(x_hbm.at[pl.ds(0, size)], out_ref, copy_sem.at[0])
    load.start()
    count = y_in.shape[0]
    batches = count // OB
    scale = 1.0 / (members - 1.0)
    code = rows_c[...]
    rows_x[...] = ((code >> 17) - span_x).astype(F32)
    rows_y[...] = (((code >> 7) & 1023) - span_y).astype(F32)
    reach = (code & 127).astype(F32)
    rows_r[...] = 1.0 / (reach * reach)
    y_ref[...] = y_in[...] * rows_i[...]
    cur_ref[...] = y_ref[pl.ds(0, OB), :]
    lane = lax.broadcasted_iota(jnp.int32, (OB, 2 * OB), 1)
    row = lax.broadcasted_iota(jnp.int32, (OB, 2 * OB), 0)
    upper = lane >= OB
    eye = jnp.where((lane == row) | (lane == row + OB), 1.0, 0.0).astype(F32)
    ys = lax.broadcasted_iota(jnp.int32, (block_y, 1), 0).astype(F32)
    none = jnp.zeros((OB, 2 * members), BF16)

    def rho_rows(at, px, py, ir):
        dx = rows_x[at, :] - px
        dy = rows_y[at, :] - py
        near = jnp.maximum(1.0 - (dx * dx + dy * dy) * ir, 0.0)
        return near * near

    def fold(x):
        return x[:, :members] + x[:, members:]

    def cells(n):
        px, py, ir = both_ref[pl.ds(0, 1), :], both_ref[pl.ds(1, 1), :], both_ref[pl.ds(2, 1), :]
        dy = ys - py
        dy2 = dy * dy * ir
        rhos = []
        for u in range(6):
            dx = jnp.float32(n * 6 + u) - px
            near = jnp.maximum((1.0 - dx * dx * ir) - dy2, 0.0)
            rhos.append((near * near)[None, None])
        rho = jnp.concatenate(rhos, axis=0)
        rows = 6 * levels * block_y
        at = pl.ds(n * rows, rows)
        flat = (rows, members)
        tall = (6, levels, block_y, members)
        old = out_ref[at, :]
        raw = project(pair_ref[...], old)
        g = (raw.reshape(tall) * rho).reshape(flat)
        raw = raw + fold(jnp.dot(wide(g), mix_ref[...], preferred_element_type=F32))
        g = (raw.reshape(tall) * rho).reshape(flat)
        new = old + fold(jnp.dot(wide(g), back_ref[...], preferred_element_type=F32))
        out_ref[at, :] = new
        return at

    def step(first, blocks, odd, b):
        fresh = b is None
        b = 0 if fresh else b
        now = pl.ds(hinted(b * OB), OB)
        after = pl.ds(hinted(jnp.minimum(b + 1, batches - 1) * OB), OB)
        pieces = []
        if not fresh:
            side0, solved0 = side_ref[...], solved_ref[...]
            px0, py0, ir0 = lanes_ref[pl.ds(0, 1), :], lanes_ref[pl.ds(1, 1), :], lanes_ref[pl.ds(2, 1), :]

            def later(start, size):
                at = pl.ds(start, size)
                old = y_ref[at, :]
                y_ref[at, :] = old + spread(solved0, project(side0, old) * rho_rows(at, px0, py0, ir0))

            for start in range((first + 1) * OB, count, 1024):
                pieces.append(functools.partial(later, start, min(1024, count - start)))
        ahead_of = len(pieces)
        for n in blocks:
            pieces.append(functools.partial(cells, n))
        plan = list([0.3, 0.6, 0.8, 1, 1, 1, 1] if odd else [0.3, 0.6, 0.8, 1, 1, 1, 1])
        total = len(pieces)
        done = [0]

        def fill():
            share = plan.pop(0)
            upto = total if not plan else min(total, round(share * total))
            while done[0] < upto:
                pieces[done[0]]()
                done[0] += 1

        hx = cur_ref[...]
        centred = hx - jnp.mean(hx, axis=1, keepdims=True)
        high, low = split(centred)
        high2 = jnp.concatenate([high, high], axis=1)
        low2 = jnp.concatenate([low, low], axis=1)
        side = jnp.concatenate([high2, low2, low2, high2], axis=0)
        fill()
        p = project(side, centred) * scale
        fill()
        norm = jnp.max(jnp.sum(jnp.abs(p), axis=0, keepdims=True), axis=1, keepdims=True)
        rhs = w_ref[now, :] - hx
        r, v, t = begin(p, rhs, norm, eye)
        for i in range(4):
            r, v, t = sharpen(r, v, t, eye, i + 1 == 4)
            fill()
            if i == 2:
                while done[0] < ahead_of:
                    pieces[done[0]]()
                    done[0] += 1
                ahead = y_ref[after, :]
                px = jnp.sum(rows_x[now, :] * eye, axis=0, keepdims=True)
                py = jnp.sum(rows_y[now, :] * eye, axis=0, keepdims=True)
                ir = jnp.sum(rows_r[now, :] * eye, axis=0, keepdims=True)
                g = project(side, ahead) * rho_rows(after, px, py, ir)
                if odd:
                    mix = project(side, first_ref[...])

        def settle(v):
            solved = stack_solved(v, scale)
            cur_ref[...] = ahead + spread(solved, g)
            solved_ref[...] = solved
            if odd:
                bh = jnp.concatenate([solved0[:OB], solved[:OB]], axis=0)
                bl = jnp.concatenate([solved0[OB : 2 * OB], solved[OB : 2 * OB]], axis=0)
                half = jnp.concatenate([bh, bl], axis=1)
                back_ref[...] = jnp.concatenate([half, half], axis=0)
            else:
                first_ref[...] = v * scale

        fill()
        settle(v)
        side_ref[...] = side
        lanes_ref[pl.ds(0, 1), :] = px
        lanes_ref[pl.ds(1, 1), :] = py
        lanes_ref[pl.ds(2, 1), :] = ir
        if odd:
            pair_ref[...] = jnp.concatenate([side0[:OB], high2, side0[OB : 2 * OB], low2], axis=0)
            mh, ml = split(jnp.where(upper, mix, 0.0))
            mrow = jnp.concatenate([mh, ml], axis=1)
            mix_ref[...] = jnp.concatenate([mrow, none, mrow, none], axis=0)
            low_half = ~upper[:1, :]
            both_ref[pl.ds(0, 1), :] = jnp.where(low_half, px0, px)
            both_ref[pl.ds(1, 1), :] = jnp.where(low_half, py0, py)
            both_ref[pl.ds(2, 1), :] = jnp.where(low_half, ir0, ir)

        @pl.when(jnp.max(norm) > QUICK)
        def _():
            t_ref[...] = p + eye
            v_ref[...] = rhs

            @pl.when(jnp.max(norm) <= WIDE)
            def _():
                r, v, t = begin(p, rhs, norm, eye)
                for i in range(LONG):
                    r, v, t = sharpen(r, v, t, eye, i + 1 == LONG)
                v_ref[...] = v

            @pl.when(jnp.max(norm) > WIDE)
            def _():
                lax.fori_loop(0, OB, pivot, 0)

            settle(v_ref[...])

    def pivot(k, _):
        trow = t_ref[pl.ds(k, 1), :]
        here = lane[:1, :] == k
        inverse = 1.0 / jnp.sum(jnp.where(here, trow, 0.0), axis=1, keepdims=True)
        trow = trow * inverse
        vrow = v_ref[pl.ds(k, 1), :] * inverse
        mat = t_ref[...]
        col = jnp.sum(jnp.where(lane == k, mat, 0.0), axis=1, keepdims=True)
        mine = row == k
        t_ref[...] = jnp.where(mine, trow, mat - col * trow)
        v_ref[...] = jnp.where(mine, vrow, v_ref[...] - col * vrow)
        return 0

    groups = block_x // 6
    early, late = range(groups // 2), range(groups // 2, groups)
    step(0, (), False, None)
    step(0, (), True, 1)

    def two(first, q, _):
        step(first, early, False, 2 * q)
        step(first, late, True, 2 * q + 1)
        return 0

    load.wait()
    two(0, 1, 0)
    for first in range(4, batches, 4):
        lax.fori_loop(first // 2, min(first + 4, batches) // 2, functools.partial(two, first), 0)
    stores = []
    for n in range(groups):
        at = cells(n)
        stores.append(pltpu.make_async_copy(out_ref.at[at], out_hbm.at[at], copy_sem.at[1 + n]))
        stores[-1].start()
    for store in stores:
        store.wait()


def run_assimilate(shape, spans, *args):
    vmem = pl.BlockSpec(memory_space=pltpu.VMEM)
    hbm = pl.BlockSpec(memory_space=pl.ANY)
    count, members = args[0].shape
    size = shape[0] * shape[1] * shape[2]
    out = pl.pallas_call(
        functools.partial(assimilate, *spans, shape),
        out_shape=jax.ShapeDtypeStruct((size, members), F32),
        in_specs=[vmem] * (len(args) - 1) + [hbm],
        out_specs=hbm,
        scratch_shapes=[
            pltpu.VMEM((count, members), F32),
            pltpu.VMEM((count, members), F32),
            pltpu.VMEM((count, members), F32),
            pltpu.VMEM((count, members), F32),
            pltpu.VMEM((OB, 2 * OB), F32),
            pltpu.VMEM((OB, members), F32),
            pltpu.VMEM((OB, members), F32),
            pltpu.VMEM((4 * OB, 2 * members), BF16),
            pltpu.VMEM((4 * OB, members), BF16),
            pltpu.VMEM((8, members), F32),
            pltpu.VMEM((OB, members), F32),
            pltpu.VMEM((4 * OB, 2 * members), BF16),
            pltpu.VMEM((4 * OB, 2 * members), BF16),
            pltpu.VMEM((4 * OB, 2 * members), BF16),
            pltpu.VMEM((8, members), F32),
            pltpu.VMEM((size, members), F32),
            pltpu.SemaphoreType.DMA((1 + shape[0] // 6,)),
        ],
        name="assimilate",
    )(*args)
    return out.reshape(shape)


def per_device(
    ensemble,
    cfl_ratio_primary_axis,
    cfl_ratio_secondary_axis,
    spreading_ratio,
    obs_owner,
    obs_local,
    batch_order,
    obs_reach,
    obs_value,
    obs_variance,
    obs_noise,
):
    block_x, block_y, levels, members = ensemble.shape
    span_x, span_y = lax.axis_size("gx"), lax.axis_size("gy")
    span = span_x * span_y
    count = obs_local.shape[0]
    size = block_x * levels * block_y
    strip = levels * block_y
    lines = block_x * levels
    flat = jnp.transpose(ensemble, (0, 2, 1, 3)).reshape(size, members)
    plane = (levels * block_x, block_y)
    coefs = [
        jnp.transpose(c, (2, 0, 1)).reshape(plane)
        for c in (cfl_ratio_primary_axis, cfl_ratio_secondary_axis, spreading_ratio)
    ]
    tile = (count // 128, 128)
    tables = [v.reshape(tile) for v in (obs_owner, obs_local, obs_reach, obs_value, obs_variance)]
    vmem = pl.BlockSpec(memory_space=pltpu.VMEM)
    smem = pl.BlockSpec(memory_space=pltpu.SMEM)
    hbm = pl.BlockSpec(memory_space=pl.ANY)
    chips = span // 2
    table = jax.ShapeDtypeStruct((count, members), F32)
    codes = jax.ShapeDtypeStruct((count, members), jnp.int32)
    full = pltpu.VMEM((count, members), F32)
    state, seen, wanted, rows_c, rows_i = pl.pallas_call(
        exchange,
        out_shape=[jax.ShapeDtypeStruct((size + 8, members), F32), table, table, codes, table],
        in_specs=[vmem] * 9 + [smem, hbm],
        out_specs=[hbm, vmem, hbm, hbm, hbm],
        scratch_shapes=[
            pltpu.VMEM((size + 8, members), F32),
            pltpu.VMEM((size, members), F32),
            pltpu.VMEM((5, size, members), F32),
            pltpu.VMEM((block_x * block_y, 128), F32),
            pltpu.VMEM((2, 2, lines, members), F32),
            pltpu.VMEM((2, 2, strip, members), F32),
            pltpu.VMEM((2, 2, lines, members), F32),
            full,
            full,
            pltpu.VMEM((count, members), jnp.int32),
            full,
            full,
            pltpu.VMEM((count // 2, members), F32),
            pltpu.VMEM((chips, count // span, members), F32),
            pltpu.VMEM((chips, count // span, members), F32),
            pltpu.VMEM((2, *tile), jnp.int32),
            pltpu.VMEM((2, *tile), F32),
            pltpu.SMEM((count,), jnp.int32),
            pltpu.SMEM((count,), jnp.int32),
            pltpu.SMEM((count,), F32),
            pltpu.SMEM((count,), F32),
            pltpu.SemaphoreType.DMA((2, 4)),
            pltpu.SemaphoreType.DMA((2, 4)),
            pltpu.SemaphoreType.DMA((4,)),
            pltpu.SemaphoreType.DMA((4,)),
            pltpu.SemaphoreType.DMA((5,)),
            pltpu.SemaphoreType.DMA((4, count // 128)),
        ],
        compiler_params=pltpu.CompilerParams(collective_id=0, has_side_effects=True),
        name="exchange",
    )(flat, *coefs, *tables, batch_order, obs_noise)
    shape = (block_x, levels, block_y, members)
    spans = (span_x * block_x, span_y * block_y)
    out = run_assimilate(shape, spans, rows_c, rows_i, seen, wanted, state)
    return jnp.transpose(out, (0, 2, 1, 3))


def solution(mesh):
    return jax.shard_map(
        per_device,
        mesh=mesh,
        in_specs=(
            P("gx", "gy", None, None),
            P("gx", "gy", None),
            P("gx", "gy", None),
            P("gx", "gy", None),
            P(),
            P(),
            P(),
            P(),
            P(),
            P(),
            P(),
        ),
        out_specs=P("gx", "gy", None, None),
        check_vma=False,
    )
```

profile of v0, /device:TPU:1, one launch (start us, length us, event | category | flops | bytes accessed | tf_op | source)
XLA Modules:
  0.0 74.6 jit_solution(18043979847612700946)
XLA Ops:
  0.0 44.1 %exchange.1 = (f32[3464,128]{1,0:T(8,128)}, f32[1024,128]{1,0:T(8,128)}, f32[1024,128]{1,0:T(8,128)}, s32[1024,128]{1,0:T(8,128)}, f32[1024,128]{1,0:T(8,128)}) custom-call(f32[3456,128]{1,0:T(8,128)} %bitcast.20, f32[144,24]{1,0:T(8,128)} %bitcast.21, f32[144,24]{1,0:T(8,128)} %bitcast.22, f32[144,24]{1,0:T(8,128)} %bitcast.23, s32[8,128]{1,0:T(8,128)} %bitcast.24, ...), custom_call_target="tpu_custom_call" | custom-call | tf_op jit(solution)/shard_map/exchange/pallas_call | solution.py:629
  44.1 30.4 %assimilate.1 = f32[3456,128]{1,0:T(8,128)} custom-call(s32[1024,128]{1,0:T(8,128)} %get-tuple-element.10.rows_c, f32[1024,128]{1,0:T(8,128)} %get-tuple-element.11.rows_i, f32[1024,128]{1,0:T(8,128)} %get-tuple-element.12.y_in, f32[1024,128]{1,0:T(8,128)} %get-tuple-element.13.w_ref, f32[3464,128]{1,0:T(8,128)} %get-tuple-element.14.x_hbm), custom_call_target="tpu_custom_call" | custom-call | tf_op jit(solution)/shard_map/assimilate/pallas_call | solution.py:565
where the time goes:
time: 75.5 us; the launch traced here: 74.6 us
  Pallas kernels  74.5 us (99%)
    pallas_call x1, Pallas kernels, per_device(): pl.pallas_call(exchange, out_shape=[jax.ShapeDtypeStruct((size + 8, membe...  44.1 us
    pallas_call x1, Pallas kernels, run_assimilate(): pl.pallas_call(functools.partial(assimilate, *spans, shape), out_shape=ja...  30.4 us

commit v1 on v0

--- a/solution.py
+++ b/solution.py
@@ -34,8 +34,8 @@
     x_ref, cx_ref, cy_ref, kd_ref, owner_ref, local_ref, reach_ref, value_ref, variance_ref, order_ref, noise_hbm,
     state_hbm, y_ref, w_hbm, rows_c_hbm, rows_i_hbm,
     field_ref, mid_ref, wide_ref, flip_ref, cols_ref, rows_in, cols_in,
-    noise_ref, w_ref, rows_c, rows_i, part_ref, half_ref, sum_ref, slots_ref, ints_ref, floats_ref,
-    place_s, code_s, inv_s, shift_s, halo_send, halo_recv, send_sem, recv_sem, copy_sem, table_sem,
+    noise_ref, w_ref, rows_c, rows_i, part_ref, half_ref, sum_ref, slots_ref, code_ref, inv_ref, place_ref,
+    place_s, spot_s, halo_send, halo_recv, send_sem, recv_sem, copy_sem, table_sem, line_recv, share_send, share_recv, step_sem,
 ):
     strip, members = rows_in.shape[2:]
     block_y = cx_ref.shape[1]
@@ -61,7 +61,7 @@
             ox = lax.rem(gx + a, nx)
             for b in range(start, my):
                 oy = lax.rem(gy // 2 + b, my)
-                visit(ox * my + oy, (ox, oy * 2 + core))
+                visit(a, ox * my + oy, (ox, oy * 2 + core))
 
         line(0, 1)
 
@@ -73,12 +73,32 @@
 
     barrier = pltpu.get_barrier_semaphore()
 
-    def greet(_, device):
+    side_x = lax.rem(gx, 2)
+    rings = nx // 2
+    columns = my // 2
+    at_z, at_x, at_y = gx // 2, gy // my, lax.rem(gy, my) // 2
+
+    def near_by(dz, flip_high, flip_low, dy):
+        high = 1 - side_x if flip_high else side_x
+        low = 1 - at_x if flip_low else at_x
+        z = lax.rem(at_z + dz + rings, rings)
+        y = lax.rem(at_y + dy + columns, columns)
+        return (z * 2 + high, low * my + y * 2 + core)
+
+    up, down = near_by(1, 0, 0, 0), near_by(-1, 0, 0, 0)
+    ahead_y, behind_y = near_by(0, 0, 0, 1), near_by(0, 0, 0, -1)
+    across, beside = near_by(0, 1, 0, 0), near_by(0, 0, 1, 0)
+    greeted = (west, east, south, north, partner, up, down, ahead_y, behind_y, across, beside)
+    for device in greeted:
         pl.semaphore_signal(barrier, inc=1, device_id=device, device_id_type=MESH)
 
-    for device in (west, east, south, north, partner):
-        greet(None, device)
-    others(greet)
+    def tell(step, devices):
+        for device in devices:
+            pl.semaphore_signal(step_sem.at[step], inc=1, device_id=device, device_id_type=MESH)
+
+    def hear(step, signals):
+        pl.semaphore_wait(step_sem.at[step], signals)
+
     fetch = pltpu.make_async_copy(noise_hbm, noise_ref, copy_sem.at[0])
     fetch.start()
     from_west = jnp.where(gx > 0, 1.0, 0.0).astype(F32)
@@ -148,10 +168,11 @@
             target[rows, :] = target[rows, :] + wide_ref[3 + side, rows, :] * (cols_in[turn, side] * here)
 
     pack(x_ref, 0)
-    pl.semaphore_wait(barrier, chips + 4)
+    pl.semaphore_wait(barrier, len(greeted))
     first = sends(x_ref, 0)
     for copy in first:
         copy.start()
+    tell(0, (beside,))
 
     def flip(i, _):
         rows = pl.ds(i, levels, stride=block_x)
@@ -165,6 +186,8 @@
         return 0
 
     lax.fori_loop(0, block_x, flip, 0, unroll=4)
+    hear(0, 1)
+    tell(1, (ahead_y, behind_y))
     kinds = 5 * levels
     r = lax.broadcasted_iota(jnp.int32, (3 * kinds, members), 0)
     pick = [((r == k) | (r == k + kinds) | (r == k + 2 * kinds)).astype(F32).astype(BF16) for k in range(kinds)]
@@ -191,52 +214,62 @@
     ox = floor_div(owner, ny, nx * ny)
     oy = owner - ox * ny
     mine = owner == gx * ny + gy
-    ints_ref[0] = jnp.where(mine, (ix * levels + lev) * block_y + iy, size)
+    place_ref[...] = jnp.where(mine, (ix * levels + lev) * block_y + iy, size)
     px = (ox - gx) * block_x + ix + nx * block_x
     py = (oy - gy) * block_y + iy + ny * block_y
-    ints_ref[1] = (px * 1024 + py) * 128 + reach_ref[...]
+    code = ((px * 1024 + py) * 128 + reach_ref[...]).T
     inv = lax.rsqrt(variance_ref[...])
-    floats_ref[0] = inv
-    floats_ref[1] = value_ref[...] * inv
     field_ref[pl.ds(size, 8), :] = jnp.zeros((8, members), F32)
-    width = ints_ref.shape[2]
+    shift = (value_ref[...] * inv).T
+    inv = inv.T
+    width = place_ref.shape[1]
     tables = [
-        pltpu.make_async_copy(source.at[r], target.at[pl.ds(r * width, width)], table_sem.at[i, r])
-        for i, (source, target) in enumerate(
-            ((ints_ref.at[0], place_s), (ints_ref.at[1], code_s), (floats_ref.at[0], inv_s), (floats_ref.at[1], shift_s))
-        )
+        pltpu.make_async_copy(place_ref.at[r], place_s.at[pl.ds(r * width, width)], table_sem.at[r])
         for r in range(count // width)
     ]
     for table in tables:
         table.start()
+    hear(1, 2)
+    tell(2, (ahead_y,))
     inside(x_ref, mid_ref)
     border(first, x_ref, mid_ref, 0)
     pack(mid_ref, 1)
     second = sends(mid_ref, 1)
     for copy in second:
         copy.start()
+    hear(2, 1)
+    tell(3, (up, down))
     inside(mid_ref, field_ref)
+    hear(3, 2)
+    tell(4, (up,))
     fetch.wait()
     for table in tables:
         table.wait()
-    full = (1, members)
-
-    def look(ref, o):
-        return ref[o]
+    for d in range(count // width):
+        rows = pl.ds(d * width, width)
+        code_ref[rows, :] = jnp.broadcast_to(code[:, d : d + 1], (width, members))
+        inv_ref[rows, :] = jnp.broadcast_to(inv[:, d : d + 1], (width, members))
+        noise_ref[rows, :] = noise_ref[rows, :] + jnp.broadcast_to(shift[:, d : d + 1], (width, members))
+
+    def spot(g, _):
+        for u in range(8):
+            spot_s[g * 8 + u] = place_s[order_ref[g * 8 + u]]
+        return 0
+
+    groups = count // 8
+    lax.fori_loop(0, groups, spot, 0)
 
     def prepare(g, _):
         for u in range(8):
-            k = g * 8 + u
-            o = order_ref[k]
-            at = pl.ds(k, 1)
-            w_ref[at, :] = noise_ref[pl.ds(o, 1), :] + jnp.full(full, look(shift_s, o))
-            rows_c[at, :] = jnp.full(full, look(code_s, o))
-            rows_i[at, :] = jnp.full(full, look(inv_s, o))
+            at = pl.ds(g * 8 + u, 1)
+            o = pl.ds(order_ref[g * 8 + u], 1)
+            w_ref[at, :] = noise_ref[o, :]
+            rows_c[at, :] = code_ref[o, :]
+            rows_i[at, :] = inv_ref[o, :]
         return 0
 
-    groups = count // 8
-    lax.fori_loop(0, groups // 8, prepare, 0)
     border(second, mid_ref, field_ref, 1)
+    hear(4, 1)
     keep = pltpu.make_async_copy(field_ref, state_hbm, copy_sem.at[0])
     keep.start()
 
@@ -244,7 +277,7 @@
         def body(g, _):
             for u in range(8):
                 k = base + g * 8 + u
-                part_ref[pl.ds(k, 1), :] = field_ref[pl.ds(look(place_s, order_ref[k]), 1), :]
+                part_ref[pl.ds(k, 1), :] = field_ref[pl.ds(spot_s[k], 1), :]
             return 0
 
         lax.fori_loop(0, half // 8, body, 0)
@@ -261,7 +294,7 @@
     swap.wait_recv()
     sum_ref[...] = (part_ref[mine, :] + half_ref[...]).reshape(sum_ref.shape)
 
-    def scatter(t, device):
+    def scatter(a, t, device):
         pltpu.make_async_remote_copy(
             src_ref=sum_ref.at[t], dst_ref=slots_ref.at[chip], send_sem=send_sem.at[1], recv_sem=recv_sem.at[1],
             device_id=device, device_id_type=MESH,
@@ -269,15 +302,15 @@
 
     others(scatter)
     slots_ref[chip] = sum_ref[chip]
-    lax.fori_loop(groups // 8, groups // 2, prepare, 0)
+    lax.fori_loop(0, groups // 2, prepare, 0)
     some = slots_ref.at[pl.ds(0, chips - 1)]
     pltpu.make_async_copy(some, some, recv_sem.at[1]).wait()
     own = pl.ds(pl.multiple_of(core * half + chip * piece, piece), piece)
     y_ref[own, :] = jnp.sum(slots_ref[...], axis=0)
 
-    def gather(t, device):
+    def gather(a, t, device):
         pltpu.make_async_remote_copy(
-            src_ref=y_ref.at[own], dst_ref=y_ref.at[own], send_sem=send_sem.at[2], recv_sem=recv_sem.at[2],
+            src_ref=y_ref.at[own], dst_ref=y_ref.at[own], send_sem=send_sem.at[2], recv_sem=line_recv.at[a],
             device_id=device, device_id_type=MESH,
         ).start()
 
@@ -289,12 +322,27 @@
     ]
     for store in stores:
         store.start()
-    pltpu.make_async_copy(some, some, recv_sem.at[2]).wait()
-    share = pltpu.make_async_remote_copy(
-        src_ref=y_ref.at[mine], dst_ref=y_ref.at[mine], send_sem=send_sem.at[3], recv_sem=recv_sem.at[3],
-        device_id=partner, device_id_type=MESH,
-    )
-    share.start()
+    block = my * piece
+
+    def share(a):
+        ox = lax.rem(gx + nx - a, nx)
+        rows = pl.ds(pl.multiple_of(core * half + ox * block, block), block)
+        return pltpu.make_async_remote_copy(
+            src_ref=y_ref.at[rows], dst_ref=y_ref.at[rows], send_sem=share_send.at[a], recv_sem=share_recv.at[a],
+            device_id=partner, device_id_type=MESH,
+        )
+
+    near = y_ref.at[pl.ds(0, block - piece)]
+    pltpu.make_async_copy(near, near, line_recv.at[0]).wait()
+    share(0).start()
+    row_block = y_ref.at[pl.ds(0, block)]
+
+    def pass_on(a, _):
+        pltpu.make_async_copy(row_block, row_block, line_recv.at[a]).wait()
+        share(a).start()
+        return 0
+
+    lax.fori_loop(1, nx, pass_on, 0)
     for copy in first + second:
         copy.wait_send()
     swap.wait_send()
@@ -303,7 +351,12 @@
         store.wait()
     pltpu.make_async_copy(some, some, send_sem.at[1]).wait()
     pltpu.make_async_copy(some, some, send_sem.at[2]).wait()
-    share.wait()
+
+    def finish(a, _):
+        share(a).wait()
+        return 0
+
+    lax.fori_loop(0, nx, finish, 0)
 
 
 def split(x):
@@ -647,18 +700,21 @@
             pltpu.VMEM((count // 2, members), F32),
             pltpu.VMEM((chips, count // span, members), F32),
             pltpu.VMEM((chips, count // span, members), F32),
-            pltpu.VMEM((2, *tile), jnp.int32),
-            pltpu.VMEM((2, *tile), F32),
+            pltpu.VMEM((count, members), jnp.int32),
+            full,
+            pltpu.VMEM(tile, jnp.int32),
             pltpu.SMEM((count,), jnp.int32),
             pltpu.SMEM((count,), jnp.int32),
-            pltpu.SMEM((count,), F32),
-            pltpu.SMEM((count,), F32),
             pltpu.SemaphoreType.DMA((2, 4)),
             pltpu.SemaphoreType.DMA((2, 4)),
             pltpu.SemaphoreType.DMA((4,)),
             pltpu.SemaphoreType.DMA((4,)),
             pltpu.SemaphoreType.DMA((5,)),
-            pltpu.SemaphoreType.DMA((4, count // 128)),
+            pltpu.SemaphoreType.DMA((count // 128,)),
+            pltpu.SemaphoreType.DMA((span_x,)),
+            pltpu.SemaphoreType.DMA((span_x,)),
+            pltpu.SemaphoreType.DMA((span_x,)),
+            pltpu.SemaphoreType.REGULAR((5,)),
         ],
         compiler_params=pltpu.CompilerParams(collective_id=0, has_side_effects=True),
         name="exchange",

time: 75.5 us -> 72.2 us (0.956); the launches traced: 74.6 us -> 72.3 us
  Pallas kernels: 74.5 us -> 72.1 us
    pallas_call x1, Pallas kernels: 44.1 us -> 41.8 us  [per_device(): pl.pallas_call(exchange, out_shape=[jax.ShapeDtypeStruct((size + 8, membe...]
where the time goes in v1:
time: 72.2 us; the launch traced here: 72.3 us
  Pallas kernels  72.1 us (100%)
    pallas_call x1, Pallas kernels, per_device(): pl.pallas_call(exchange, out_shape=[jax.ShapeDtypeStruct((size + 8, membe...  41.8 us
    pallas_call x1, Pallas kernels, run_assimilate(): pl.pallas_call(functools.partial(assimilate, *spans, shape), out_shape=ja...  30.3 us

profile of v1, /device:TPU:1, one launch (start us, length us, event | category | flops | bytes accessed | tf_op | source)
XLA Modules:
  0.0 72.3 jit_solution(14674342689896757371)
XLA Ops:
  0.0 41.8 %exchange.1 = (f32[3464,128]{1,0:T(8,128)}, f32[1024,128]{1,0:T(8,128)}, f32[1024,128]{1,0:T(8,128)}, s32[1024,128]{1,0:T(8,128)}, f32[1024,128]{1,0:T(8,128)}) custom-call(f32[3456,128]{1,0:T(8,128)} %bitcast.20, f32[144,24]{1,0:T(8,128)} %bitcast.21, f32[144,24]{1,0:T(8,128)} %bitcast.22, f32[144,24]{1,0:T(8,128)} %bitcast.23, s32[8,128]{1,0:T(8,128)} %bitcast.24, ...), custom_call_target="tpu_custom_call" | custom-call | tf_op jit(solution)/shard_map/exchange/pallas_call | solution.py:682
  41.8 30.3 %assimilate.1 = f32[3456,128]{1,0:T(8,128)} custom-call(s32[1024,128]{1,0:T(8,128)} %get-tuple-element.10.rows_c, f32[1024,128]{1,0:T(8,128)} %get-tuple-element.11.rows_i, f32[1024,128]{1,0:T(8,128)} %get-tuple-element.12.y_in, f32[1024,128]{1,0:T(8,128)} %get-tuple-element.13.w_ref, f32[3464,128]{1,0:T(8,128)} %get-tuple-element.14.x_hbm), custom_call_target="tpu_custom_call" | custom-call | tf_op jit(solution)/shard_map/assimilate/pallas_call | solution.py:618

commit v2 on v1

--- a/solution.py
+++ b/solution.py
@@ -8,6 +8,7 @@
 from jax.sharding import PartitionSpec as P
 
 OB = 64
+SWAPS = 2
 QUICK = 6.5
 WIDE = 63.0
 LONG = 6
@@ -31,11 +32,11 @@
 
 
 def exchange(
-    x_ref, cx_ref, cy_ref, kd_ref, owner_ref, local_ref, reach_ref, value_ref, variance_ref, order_ref, noise_hbm,
+    x_hbm, cx_ref, cy_ref, kd_ref, owner_ref, local_ref, reach_ref, value_ref, variance_ref, order_ref, noise_hbm,
     state_hbm, y_ref, w_hbm, rows_c_hbm, rows_i_hbm,
     field_ref, mid_ref, wide_ref, flip_ref, cols_ref, rows_in, cols_in,
     noise_ref, w_ref, rows_c, rows_i, part_ref, half_ref, sum_ref, slots_ref, code_ref, inv_ref, place_ref,
-    place_s, spot_s, halo_send, halo_recv, send_sem, recv_sem, copy_sem, table_sem, line_recv, share_send, share_recv, step_sem,
+    place_s, spot_s, halo_send, halo_recv, send_sem, recv_sem, copy_sem, table_sem, line_recv, share_send, share_recv, step_sem, x_ref, load_sem, swap_send, swap_recv,
 ):
     strip, members = rows_in.shape[2:]
     block_y = cx_ref.shape[1]
@@ -92,6 +93,9 @@
     for device in greeted:
         pl.semaphore_signal(barrier, inc=1, device_id=device, device_id_type=MESH)
 
+    load = pltpu.make_async_copy(x_hbm, x_ref, load_sem)
+    load.start()
+
     def tell(step, devices):
         for device in devices:
             pl.semaphore_signal(step_sem.at[step], inc=1, device_id=device, device_id_type=MESH)
@@ -167,12 +171,15 @@
             rows = pl.ds(at, lines, stride=block_y)
             target[rows, :] = target[rows, :] + wide_ref[3 + side, rows, :] * (cols_in[turn, side] * here)
 
-    pack(x_ref, 0)
     pl.semaphore_wait(barrier, len(greeted))
-    first = sends(x_ref, 0)
-    for copy in first:
+    first = sends(x_hbm, 0)
+    for copy in first[:2]:
         copy.start()
     tell(0, (beside,))
+    load.wait()
+    pack(x_ref, 0)
+    for copy in first[2:]:
+        copy.start()
 
     def flip(i, _):
         rows = pl.ds(i, levels, stride=block_x)
@@ -273,25 +280,31 @@
     keep = pltpu.make_async_copy(field_ref, state_hbm, copy_sem.at[0])
     keep.start()
 
-    def pick_rows(base):
+    def pick_rows(base, rows):
         def body(g, _):
             for u in range(8):
                 k = base + g * 8 + u
                 part_ref[pl.ds(k, 1), :] = field_ref[pl.ds(spot_s[k], 1), :]
             return 0
 
-        lax.fori_loop(0, half // 8, body, 0)
+        lax.fori_loop(0, rows // 8, body, 0)
 
     mine = pl.ds(pl.multiple_of(core * half, half), half)
-    other = pl.ds(pl.multiple_of((1 - core) * half, half), half)
-    pick_rows((1 - core) * half)
-    swap = pltpu.make_async_remote_copy(
-        src_ref=part_ref.at[other], dst_ref=half_ref, send_sem=send_sem.at[0], recv_sem=recv_sem.at[0],
-        device_id=partner, device_id_type=MESH,
-    )
-    swap.start()
-    pick_rows(core * half)
-    swap.wait_recv()
+    swaps = []
+    part = half // SWAPS
+    for c in range(SWAPS):
+        base = pl.multiple_of((1 - core) * half + c * part, part)
+        pick_rows(base, part)
+        swaps.append(
+            pltpu.make_async_remote_copy(
+                src_ref=part_ref.at[pl.ds(base, part)], dst_ref=half_ref.at[pl.ds(c * part, part)],
+                send_sem=swap_send.at[c], recv_sem=swap_recv.at[c], device_id=partner, device_id_type=MESH,
+            )
+        )
+        swaps[-1].start()
+    pick_rows(core * half, half)
+    for swap in swaps:
+        swap.wait_recv()
     sum_ref[...] = (part_ref[mine, :] + half_ref[...]).reshape(sum_ref.shape)
 
     def scatter(a, t, device):
@@ -345,7 +358,8 @@
     lax.fori_loop(1, nx, pass_on, 0)
     for copy in first + second:
         copy.wait_send()
-    swap.wait_send()
+    for swap in swaps:
+        swap.wait_send()
     keep.wait()
     for store in stores:
         store.wait()
@@ -682,7 +696,7 @@
     state, seen, wanted, rows_c, rows_i = pl.pallas_call(
         exchange,
         out_shape=[jax.ShapeDtypeStruct((size + 8, members), F32), table, table, codes, table],
-        in_specs=[vmem] * 9 + [smem, hbm],
+        in_specs=[hbm] + [vmem] * 8 + [smem, hbm],
         out_specs=[hbm, vmem, hbm, hbm, hbm],
         scratch_shapes=[
             pltpu.VMEM((size + 8, members), F32),
@@ -715,6 +729,10 @@
             pltpu.SemaphoreType.DMA((span_x,)),
             pltpu.SemaphoreType.DMA((span_x,)),
             pltpu.SemaphoreType.REGULAR((5,)),
+            pltpu.VMEM((size, members), F32),
+            pltpu.SemaphoreType.DMA,
+            pltpu.SemaphoreType.DMA((SWAPS,)),
+            pltpu.SemaphoreType.DMA((SWAPS,)),
         ],
         compiler_params=pltpu.CompilerParams(collective_id=0, has_side_effects=True),
         name="exchange",

time: 72.2 us -> 73.4 us (1.017); the launches traced: 72.3 us -> 72 us
  no operation moved by 1% of the time
where the time goes in v2:
time: 73.4 us; the launch traced here: 72 us
  Pallas kernels  71.9 us (98%)
    pallas_call x1, Pallas kernels, per_device(): pl.pallas_call(exchange, out_shape=[jax.ShapeDtypeStruct((size + 8, membe...  41.5 us
    pallas_call x1, Pallas kernels, run_assimilate(): pl.pallas_call(functools.partial(assimilate, *spans, shape), out_shape=ja...  30.3 us

profile of v2, /device:TPU:1, one launch (start us, length us, event | category | flops | bytes accessed | tf_op | source)
XLA Modules:
  0.0 72.0 jit_solution(16168618774508775909)
XLA Ops:
  0.0 41.5 %exchange.1 = (f32[3464,128]{1,0:T(8,128)}, f32[1024,128]{1,0:T(8,128)}, f32[1024,128]{1,0:T(8,128)}, s32[1024,128]{1,0:T(8,128)}, f32[1024,128]{1,0:T(8,128)}) custom-call(f32[3456,128]{1,0:T(8,128)} %bitcast.20, f32[144,24]{1,0:T(8,128)} %bitcast.21, f32[144,24]{1,0:T(8,128)} %bitcast.22, f32[144,24]{1,0:T(8,128)} %bitcast.23, s32[8,128]{1,0:T(8,128)} %bitcast.24, ...), custom_call_target="tpu_custom_call" | custom-call | tf_op jit(solution)/shard_map/exchange/pallas_call | solution.py:696
  41.5 30.3 %assimilate.1 = f32[3456,128]{1,0:T(8,128)} custom-call(s32[1024,128]{1,0:T(8,128)} %get-tuple-element.10.rows_c, f32[1024,128]{1,0:T(8,128)} %get-tuple-element.11.rows_i, f32[1024,128]{1,0:T(8,128)} %get-tuple-element.12.y_in, f32[1024,128]{1,0:T(8,128)} %get-tuple-element.13.w_ref, f32[3464,128]{1,0:T(8,128)} %get-tuple-element.14.x_hbm), custom_call_target="tpu_custom_call" | custom-call | tf_op jit(solution)/shard_map/assimilate/pallas_call | solution.py:632
